TPU v7x, 256 devices: a whole 4x4x8 slice. The times are simulated.
256 devices in a mesh: ctx: 64 (over x, z, y_lo), tp: 4 (over y_hi, core).
Axes of the slice: x: 4, y: 4 (y_hi: 2, y_lo: 2; y = y_hi * 2 + y_lo), z: 8, core: 2. Of those that a mesh axis runs over, the one named last changes fastest.
Arguments:
- pre: float32 [3, 1024, 16384], P(None, 'tp', 'ctx'), may hold values from -6 to 6
- raw_filter: float32 [1024, 16384], P('tp', 'ctx'), may hold values from -6 to 6
- decay: float32 [1024], P('tp'), may hold values from 0 to 1, as said below
- taps: float32 [3, 3, 1024], P(None, None, 'tp'), may hold values from -3.5 to 3.5
- grad_out: float32 [1024, 16384], P(None, ('ctx', 'tp')), may hold values from -6 to 6
Outputs:
- grad_pre: float32 [3, 1024, 16384], P(None, 'tp', 'ctx')
- grad_filter: float32 [1024, 16384], P('tp', 'ctx')
- grad_taps: float32 [3, 3, 1024], P(None, None, 'tp')
Inputs may be any that keep to these rules, and one draw needn't show every extreme that they name: `decay`: rates per token between 0.3 / 16384 and 1 / 40.
All inputs are finite; a program needn't handle non-finite values.
Results may differ from a plain program's by a relative error of at most 0.00013.
Values sent between devices are 32-bit elements; how exact they have to be, the bound alone decides.
No kernel may reach another device: no remote copies, remote signals or barrier semaphores. Data moves between devices by JAX's collectives and lax.ppermute only.
A program may use at most 128 MiB of HBM per device.

v0:
```python
import math
import jax
import jax.numpy as jnp
from jax import lax
from jax.sharding import PartitionSpec as P


def passed_along(x, axis, by):
    devices = lax.axis_size(axis)
    pairs = [(i, i + by) for i in range(devices) if 0 <= i + by < devices]
    return lax.ppermute(x, axis, pairs)


def make_tables(outer_len, inner_len):
    total_len = outer_len * inner_len
    outer_index = jnp.arange(outer_len, dtype=jnp.int32)
    inner_index = jnp.arange(inner_len, dtype=jnp.int32)
    outer_angle = (outer_index[:, None] * outer_index[None, :] % outer_len).astype(jnp.float32) * (
        2.0 * math.pi / outer_len
    )
    inner_angle = (inner_index[:, None] * inner_index[None, :] % inner_len).astype(jnp.float32) * (
        2.0 * math.pi / inner_len
    )
    twist_angle = (outer_index[:, None] * inner_index[None, :] % total_len).astype(jnp.float32) * (
        2.0 * math.pi / total_len
    )
    return (
        jnp.cos(outer_angle),
        jnp.sin(outer_angle),
        jnp.cos(inner_angle),
        jnp.sin(inner_angle),
        jnp.cos(twist_angle),
        jnp.sin(twist_angle),
    )


def matmul_inner(blocks, table):
    return jnp.einsum("ncb,be->nce", blocks, table, precision=lax.Precision.HIGHEST)


def forward_spectrum(signal, tables, outer_len, inner_len):
    cos_outer, sin_outer, cos_inner, sin_inner, cos_twist, sin_twist = tables
    half_rows = outer_len // 2
    blocks = signal.reshape(signal.shape[0], half_rows, inner_len)
    real_a = jnp.einsum(
        "ca,nab->ncb", cos_outer[:, :half_rows], blocks, precision=lax.Precision.HIGHEST
    )
    imag_a = -jnp.einsum(
        "ca,nab->ncb", sin_outer[:, :half_rows], blocks, precision=lax.Precision.HIGHEST
    )
    real_b = real_a * cos_twist + imag_a * sin_twist
    imag_b = imag_a * cos_twist - real_a * sin_twist
    real_r = matmul_inner(real_b, cos_inner) + matmul_inner(imag_b, sin_inner)
    imag_r = matmul_inner(imag_b, cos_inner) - matmul_inner(real_b, sin_inner)
    return (real_r, imag_r)


def inverse_signal(real_r, imag_r, tables, outer_len, inner_len):
    cos_outer, sin_outer, cos_inner, sin_inner, cos_twist, sin_twist = tables
    half_rows = outer_len // 2
    real_s = matmul_inner(real_r, cos_inner) - matmul_inner(imag_r, sin_inner)
    imag_s = matmul_inner(imag_r, cos_inner) + matmul_inner(real_r, sin_inner)
    real_t = real_s * cos_twist - imag_s * sin_twist
    imag_t = imag_s * cos_twist + real_s * sin_twist
    signal = jnp.einsum(
        "ac,ncb->nab", cos_outer[:half_rows], real_t, precision=lax.Precision.HIGHEST
    )
    signal = signal - jnp.einsum(
        "ac,ncb->nab", sin_outer[:half_rows], imag_t, precision=lax.Precision.HIGHEST
    )
    signal = signal * (1.0 / (outer_len * inner_len))
    return signal.reshape(signal.shape[0], half_rows * inner_len)


def long_terms(product, kernel, grad_gate, outer_len, inner_len):
    tables = make_tables(outer_len, inner_len)
    kernel_re, kernel_im = forward_spectrum(kernel, tables, outer_len, inner_len)
    product_re, product_im = forward_spectrum(product, tables, outer_len, inner_len)
    gate_re, gate_im = forward_spectrum(grad_gate, tables, outer_len, inner_len)
    mixed_long = inverse_signal(
        kernel_re * product_re - kernel_im * product_im,
        kernel_re * product_im + kernel_im * product_re,
        tables,
        outer_len,
        inner_len,
    )
    grad_product = inverse_signal(
        kernel_re * gate_re + kernel_im * gate_im,
        kernel_re * gate_im - kernel_im * gate_re,
        tables,
        outer_len,
        inner_len,
    )
    grad_kernel = inverse_signal(
        product_re * gate_re + product_im * gate_im,
        product_re * gate_im - product_im * gate_re,
        tables,
        outer_len,
        inner_len,
    )
    return (mixed_long, grad_product, grad_kernel)


def local(pre, raw_filter, decay, taps, grad_out):
    tap_count = taps.shape[1]
    reach = tap_count - 1
    tok_dev = pre.shape[2]
    ctx_count = lax.axis_size("ctx")
    seq_len = tok_dev * ctx_count
    outer_len = 4 * ctx_count
    inner_len = tok_dev // 2
    before = passed_along(pre[:, :, tok_dev - reach :], "ctx", 1)
    extended = jnp.concatenate([before, pre], axis=2)
    featured = taps[:, 0, :, None] * extended[:, :, reach : reach + tok_dev]
    for j in range(1, tap_count):
        featured = featured + taps[:, j, :, None] * extended[:, :, reach - j : reach - j + tok_dev]
    query_post, key_post, value_post = (featured[0], featured[1], featured[2])
    offset = lax.axis_index("ctx") * tok_dev
    positions = (offset + jnp.arange(tok_dev, dtype=jnp.int32)).astype(jnp.float32)
    envelope = jnp.exp(-decay[:, None] * positions[None, :]) * (1.0 / math.sqrt(seq_len))
    kernel = raw_filter * envelope
    tp_count = lax.axis_size("tp")
    sliver_width = grad_out.shape[0] // (tp_count * ctx_count)
    arranged = grad_out.reshape(tp_count, ctx_count, sliver_width, grad_out.shape[1])
    grad_sliver = lax.all_to_all(
        lax.all_to_all(arranged, "tp", split_axis=0, concat_axis=3, tiled=True),
        "ctx",
        split_axis=1,
        concat_axis=3,
        tiled=True,
    ).reshape(sliver_width, seq_len)
    packed = jnp.stack([query_post, key_post, value_post, kernel])
    slivers = lax.all_to_all(packed, "ctx", split_axis=1, concat_axis=2, tiled=True)
    product = slivers[1] * slivers[2]
    grad_gate = grad_sliver * slivers[0]
    mixed_long, grad_product, grad_kernel = long_terms(
        product, slivers[3], grad_gate, outer_len, inner_len
    )
    results = jnp.stack(
        [
            grad_sliver * mixed_long,
            grad_product * slivers[2],
            grad_product * slivers[1],
            grad_kernel,
        ]
    )
    returned = lax.all_to_all(results, "ctx", split_axis=2, concat_axis=1, tiled=True)
    grad_featured = returned[:3]
    kernel_grad_tok = returned[3]
    after = passed_along(grad_featured[:, :, :reach], "ctx", -1)
    grad_extended = jnp.concatenate([grad_featured, after], axis=2)
    grad_pre = taps[:, 0, :, None] * grad_extended[:, :, 0:tok_dev]
    for j in range(1, tap_count):
        grad_pre = grad_pre + taps[:, j, :, None] * grad_extended[:, :, j : j + tok_dev]
    tap_terms = [
        jnp.sum(grad_featured * extended[:, :, reach - j : reach - j + tok_dev], axis=2)
        for j in range(tap_count)
    ]
    local_taps = jnp.stack(tap_terms, axis=1)
    grad_taps = lax.psum(local_taps, "ctx") * (1.0 / math.sqrt(seq_len))
    grad_filter = kernel_grad_tok * envelope
    return (grad_pre, grad_filter, grad_taps)


def solution(mesh):
    in_specs = (
        P(None, "tp", "ctx"),
        P("tp", "ctx"),
        P("tp"),
        P(None, None, "tp"),
        P(None, ("ctx", "tp")),
    )
    out_specs = (P(None, "tp", "ctx"), P("tp", "ctx"), P(None, None, "tp"))
    return jax.shard_map(local, mesh=mesh, in_specs=in_specs, out_specs=out_specs, check_vma=False)
```

profile of v0, /device:TPU:16, one launch (start us, length us, event | category | flops | bytes accessed | tf_op | source)
XLA Modules:
  0.0 629.1 jit_solution(6635581628537031192)
XLA Ops:
  0.7 1.2 slice.102
  2.0 3.2 collective-permute-start
  5.2 1.1 copy.235
  6.4 1.2 reshape.148
  7.6 4.8 all-to-all-start
  12.5 4.2 all-to-all-done
  17.3 1.4 reduce
  19.4 1.0 reshape.147
  20.4 12.6 %all-to-all-start.1 = ((f32[1,64,4,256]{3,2,0,1:T(4,128)}), f32[1,64,4,256]{3,2,0,1:T(4,128)S(1)}, u32[]{:S(2)}, u32[]{:S(2)}) async-start(f32[1,64,4,256]{3,2,0,1:T(4,128)} %reshape.147), calls=%async_computation.1 | async-start | bytes 524288 | tf_op jit(solution)/shard_map/all_to_all | solution.py:125
  34.6 2.5 multiply_add_fusion
  37.1 1.5 pad_maximum_fusion.2
  38.6 6.6 %all-to-all-done.1 = f32[1,64,4,256]{3,2,0,1:T(4,128)S(1)} async-done(((f32[1,64,4,256]{3,2,0,1:T(4,128)}), f32[1,64,4,256]{3,2,0,1:T(4,128)S(1)}, u32[]{:S(2)}, u32[]{:S(2)}) %all-to-all-start.1) | async-done | bytes 262176 | tf_op jit(solution)/shard_map/all_to_all | solution.py:125
  45.2 6.2 all-to-all-start.2
  54.0 25.6 %all-to-all-done.2 = f32[4,256,256]{2,0,1:T(4,128)S(1)} async-done(((f32[4,256,256]{2,0,1:T(4,128)}), f32[4,256,256]{2,0,1:T(4,128)S(1)}, u32[]{:S(2)}, u32[]{:S(2)}) %all-to-all-start.2) | async-done | bytes 1048608 | tf_op jit(solution)/shard_map/all_to_all | solution.py:133
  83.0 1.6 convolution_bitcast_fusion
  86.0 1.6 convolution_bitcast_fusion.1
  87.6 2.0 fusion.96
  89.6 2.0 fusion.100
  91.6 2.0 fusion.88
  93.6 2.2 fusion.90
  95.8 2.0 fusion.98
  97.8 2.0 fusion.102
  99.8 1.8 squeeze.15
  101.6 1.8 squeeze.16
  103.4 2.3 convolution_subtract_fusion.4
  105.7 1.2 convolution_add_fusion.4
  107.0 1.2 convolution_subtract_fusion.2
  108.2 1.2 convolution_add_fusion.2
  109.5 1.2 convolution_add_fusion.5
  110.7 1.4 multiply_subtract_fusion.3
  112.9 1.3 fusion.92
  116.6 1.3 fusion.4
  117.9 1.1 copy.262
  130.7 20.5 %copy.280 = f32[4,4,16384]{1,0,2:T(4,128)} copy(f32[4,4,16384]{2,1,0:T(4,128)S(1)} %pad_maximum_fusion.3) | data formatting | bytes 2097152 | tf_op jit(solution)/shard_map/stack | solution.py:139
  151.1 40.5 %reshape.150 = f32[64,1,4096]{2,1,0:T(1,128)S(1)} reshape(f32[16384,4,4]{2,1,0:T(4,128)} %bitcast.144) | data formatting | bytes 2097152
  191.7 34.2 %all_to_all.63 = f32[64,1,4096]{2,1,0:T(1,128)S(1)} all-to-all(f32[64,1,4096]{2,1,0:T(1,128)S(1)} %reshape.150), channel_id=1, replica_groups=mesh['ctx'=64,'tp'=4] {'ctx'}, dimensions={0} | all-to-all | bytes 2097152 | tf_op jit(solution)/shard_map/all_to_all | solution.py:147
  225.8 3.3 reduce.1
  229.1 45.5 %reshape.151 = f32[16384,4,4]{2,1,0:T(4,128)} reshape(f32[64,4096]{1,0:T(8,128)S(1)} %reduce.1) | data formatting | bytes 2097152
  274.6 24.2 %copy.281 = f32[4,4,64,256]{3,1,2,0:T(4,128)S(1)} copy(f32[4,4,64,256]{1,0,3,2:T(4,128)} %bitcast.145) | data formatting | bytes 2097152 | tf_op jit(solution)/shard_map/all_to_all | solution.py:147
  301.2 1.2 copy.283
  302.4 1.5 collective-permute-start.1
  303.9 1.8 fusion.53
  305.7 2.4 collective-permute-done.1
  308.0 1.7 copy.284
  309.8 8.9 %multiply_reduce_fusion.1 = (f32[3,256]{0,1:T(8,128)}, f32[3,256]{0,1:T(8,128)}, f32[3,256]{0,1:T(8,128)}, f32[3,256,256]{2,0,1:T(4,128)}) fusion(f32[3,256,256]{2,0,1:T(4,128)S(1)} %bitcast.147, f32[3,256,256]{2,0,1:T(4,128)S(1)} %copy-done.1, f32[3,256,2]{2,0,1:T(4,128)S(1)} %copy-done.5, f32[3,256,256]{2,1,0:T(8,128)S(1)} %copy-done.3, ...), kind=kLoop, calls=%fused_computation.46 | loop fusion | flops 2946816 | bytes 3176448 | tf_op jit(solution)/shard_map/reduce_sum | solution.py:156
  319.6 1.0 copy.288
  321.6 304.4 %psum.7 = f32[3,3,256]{2,0,1:T(4,128)S(1)} all-reduce(f32[3,3,256]{2,0,1:T(4,128)S(1)} %pad_maximum_fusion.4), channel_id=1, replica_groups=mesh['ctx'=64,'tp'=4] {'ctx'}, use_global_device_ids=true, to_apply=%region_3.4 | all-reduce | flops 2304 | bytes 18432 | tf_op jit(solution)/shard_map/psum | solution.py:160
  626.6 2.3 copy.289
  (125 shorter events, 30.0 us)
Async XLA Ops:
  0.6 11.8 %copy-start.30 = (f32[256]{0:T(256)S(1)}, f32[256]{0:T(256)}, u32[]{:S(2)}) copy-start(f32[256]{0:T(256)} %param.7) | copy-start | bytes 3076
  0.6 11.8 %copy-start.28 = (f32[256,256]{1,0:T(8,128)S(1)}, f32[256,256]{1,0:T(8,128)}, u32[]{:S(2)}) copy-start(f32[256,256]{1,0:T(8,128)} %param.6) | copy-start | bytes 786436
  2.0 32.3 %collective-permute-start = (f32[3,256,2]{1,0,2:T(4,128)S(1)}, f32[3,256,2]{1,0,2:T(4,128)S(1)}, u32[]{:S(2)}, u32[]{:S(2)}) collective-permute-start(f32[3,256,2]{1,0,2:T(4,128)S(1)} %copy.326), channel_id=1, source_target_pairs={{0,4},{4,8},{8,12},{12,16},{16,20},{20,24},{24,28},{28,32},{32,36}... | collective-permute-start | bytes 18440 | tf_op jit(solution)/shard_map/ppermute | solution.py:11
  7.6 9.2 %all-to-all-start = ((f32[4,1,16384]{2,1,0:T(1,128)}), f32[4,1,16384]{2,1,0:T(1,128)S(1)}, u32[]{:S(2)}, u32[]{:S(2)}) async-start(f32[4,1,16384]{2,1,0:T(1,128)} %reshape.148), calls=%async_computation | async-start | bytes 524288 | tf_op jit(solution)/shard_map/all_to_all | solution.py:126
  18.6 14.4 %copy-start.29 = (f32[3,3,256]{2,1,0:T(4,128)S(1)}, f32[3,3,256]{2,1,0:T(4,128)}, u32[]{:S(2)}) copy-start(f32[3,3,256]{2,1,0:T(4,128)} %param.8) | copy-start | bytes 27652
  18.7 14.4 %copy-start.2 = (f32[3,256,256]{2,1,0:T(8,128)S(1)}, f32[3,256,256]{2,1,0:T(8,128)}, u32[]{:S(2)}) copy-start(f32[3,256,256]{2,1,0:T(8,128)} %param.5) | copy-start | bytes 2359300
  20.4 24.7 %all-to-all-start.1 = ((f32[1,64,4,256]{3,2,0,1:T(4,128)}), f32[1,64,4,256]{3,2,0,1:T(4,128)S(1)}, u32[]{:S(2)}, u32[]{:S(2)}) async-start(f32[1,64,4,256]{3,2,0,1:T(4,128)} %reshape.147), calls=%async_computation.1 | async-start | bytes 524288 | tf_op jit(solution)/shard_map/all_to_all | solution.py:125
  33.6 3.5 copy-start
  33.9 3.2 copy-start.22
  34.1 3.1 copy-start.23
  34.6 4.0 copy-start.4
  45.2 8.7 %copy-start.14 = (f32[1,64,4,256]{3,2,0,1:T(4,128)}, f32[1,64,4,256]{3,2,0,1:T(4,128)S(1)}, u32[]{:S(2)}) copy-start(f32[1,64,4,256]{3,2,0,1:T(4,128)S(1)} %all-to-all-done.1) | copy-start | bytes 786436
  45.2 34.4 %all-to-all-start.2 = ((f32[4,256,256]{2,0,1:T(4,128)}), f32[4,256,256]{2,0,1:T(4,128)S(1)}, u32[]{:S(2)}, u32[]{:S(2)}) async-start(f32[4,256,256]{2,0,1:T(4,128)} %pad_maximum_fusion.2), calls=%async_computation.2 | async-start | bytes 2097152 | tf_op jit(solution)/shard_map/all_to_all | solution.py:133
  52.3 30.7 %copy-start.6 = (f32[256,256]{1,0:T(8,128)}, f32[256,256]{1,0:T(8,128)S(1)}, u32[]{:S(2)}) copy-start(f32[256,256]{1,0:T(8,128)S(1)} %fusion.61) | copy-start | bytes 786436
  53.3 31.3 %copy-start.10 = (f32[256,256]{1,0:T(8,128)}, f32[256,256]{1,0:T(8,128)S(1)}, u32[]{:S(2)}) copy-start(f32[256,256]{1,0:T(8,128)S(1)} %fusion.60) | copy-start | bytes 786436
  81.1 1.3 copy-start.16
  82.4 2.2 copy-start.27
  84.7 0.7 copy-start.13
  103.4 2.3 copy-start.20
  105.7 1.2 copy-start.19
  107.0 1.2 copy-start.17
  108.2 1.2 copy-start.18
  109.4 1.2 copy-start.21
  114.2 1.8 copy-start.7
  115.1 1.5 copy-start.11
  121.5 1.8 copy-start.8
  122.4 1.5 copy-start.12
  126.5 1.8 copy-start.9
  129.1 1.0 copy-start.15
  129.1 1.0 copy-start.26
  129.1 1.1 copy-start.24
  129.1 1.2 copy-start.25
  300.3 9.5 %copy-start.1 = (f32[3,256,256]{2,0,1:T(4,128)S(1)}, f32[3,256,256]{2,0,1:T(4,128)}, u32[]{:S(2)}) copy-start(f32[3,256,256]{2,0,1:T(4,128)} %copy-done) | copy-start | bytes 2359300
  300.3 9.5 %copy-start.3 = (f32[3,256,256]{2,1,0:T(8,128)S(1)}, f32[3,256,256]{2,1,0:T(8,128)}, u32[]{:S(2)}) copy-start(f32[3,256,256]{2,1,0:T(8,128)} %param.5) | copy-start | bytes 2359300
  300.3 9.5 %copy-start.5 = (f32[3,256,2]{2,0,1:T(4,128)S(1)}, f32[3,256,2]{2,0,1:T(4,128)}, u32[]{:S(2)}) copy-start(f32[3,256,2]{2,0,1:T(4,128)} %copy-done.4) | copy-start | bytes 18436
  302.4 5.7 collective-permute-start.1
where the time goes:
time: 636 us; the launch traced here: 629 us
  blocking collectives  339 us (53%)
  local copies, waits for them, and re-layouts  157 us (25%)
  matrix products  41.7 us (7%)
  waiting for transfers between devices  38.8 us (6%)
  starting transfers between devices  28.2 us (4%)
  other arithmetic  23.2 us (4%)
    psum x1, blocking collectives, local(): grad_taps = lax.psum(local_taps, 'ctx') * (1.0 / math.sqrt(seq_len))  304 us
    unnamed x71, local copies, waits for them, and re-layouts  93.3 us
    all_to_all x1, blocking collectives, local(): lax.all_to_all(results, 'ctx', split_axis=2, concat_axis=1, tiled=True)  34.2 us
    dot_general x24, matrix products, matmul_inner(): jnp.einsum('ncb,be->nce', blocks, table, precision=lax.Precision.HIGHEST)  31.6 us
    all_to_all x1, waiting for transfers between devices, local(): lax.all_to_all(packed, 'ctx', split_axis=1, concat_axis=2, tiled=True)  25.6 us
    all_to_all x1, local copies, waits for them, and re-layouts, local(): lax.all_to_all(results, 'ctx', split_axis=2, concat_axis=1, tiled=True)  24.2 us
    another operation x2, local copies, waits for them, and re-layouts, local(): jnp.stack([grad_sliver * mixed_long, grad_product * slivers[2], grad_prod...  20.6 us
  transfers between devices with their start and end apart: 5, of which 4 were waited for; matrix products, arithmetic and copies ran while one was open for 3% of the time, Pallas kernels for 0%

commit v1 on v0

--- a/solution.py
+++ b/solution.py
@@ -3,6 +3,11 @@
 import jax.numpy as jnp
 from jax import lax
 from jax.sharding import PartitionSpec as P
+
+
+def add_all(x, axis):
+    parts = lax.all_gather(x, axis)
+    return jnp.sum(parts, axis=0)
 
 
 def passed_along(x, axis, by):
@@ -157,7 +162,7 @@
         for j in range(tap_count)
     ]
     local_taps = jnp.stack(tap_terms, axis=1)
-    grad_taps = lax.psum(local_taps, "ctx") * (1.0 / math.sqrt(seq_len))
+    grad_taps = add_all(local_taps, "ctx") * (1.0 / math.sqrt(seq_len))
     grad_filter = kernel_grad_tok * envelope
     return (grad_pre, grad_filter, grad_taps)
 

time: 636 us -> 488 us (0.77)
  blocking collectives: 339 us -> 190 us
    psum x1 -> x0, blocking collectives: 304 us -> none  [local(): grad_taps = lax.psum(local_taps, 'ctx') * (1.0 / math.sqrt(seq_len))]
    all_gather x0 -> x1, blocking collectives: none -> 156 us  [add_all(): parts = lax.all_gather(x, axis)]
where the time goes in v1:
time: 488 us; the launch traced here: 481 us
  blocking collectives  190 us (39%)
  local copies, waits for them, and re-layouts  156 us (32%)
  matrix products  42.6 us (9%)
  waiting for transfers between devices  38.8 us (8%)
  starting transfers between devices  28.2 us (6%)
  other arithmetic  23.3 us (5%)
    all_gather x1, blocking collectives, add_all(): parts = lax.all_gather(x, axis)  156 us
    unnamed x71, local copies, waits for them, and re-layouts  91.4 us
    all_to_all x1, blocking collectives, local(): lax.all_to_all(results, 'ctx', split_axis=2, concat_axis=1, tiled=True)  34.2 us
    dot_general x24, matrix products, matmul_inner(): jnp.einsum('ncb,be->nce', blocks, table, precision=lax.Precision.HIGHEST)  31.6 us
    all_to_all x1, waiting for transfers between devices, local(): lax.all_to_all(packed, 'ctx', split_axis=1, concat_axis=2, tiled=True)  25.6 us
    all_to_all x1, local copies, waits for them, and re-layouts, local(): lax.all_to_all(results, 'ctx', split_axis=2, concat_axis=1, tiled=True)  24.2 us
    another operation x2, local copies, waits for them, and re-layouts, local(): jnp.stack([grad_sliver * mixed_long, grad_product * slivers[2], grad_prod...  20.6 us
    all_to_all x1, starting transfers between devices, local(): lax.all_to_all(lax.all_to_all(arranged, 'tp', split_axis=0, concat_axis=3...  12.6 us
  transfers between devices with their start and end apart: 5, of which 4 were waited for; matrix products, arithmetic and copies ran while one was open for 3% of the time, Pallas kernels for 0%

profile of v1, /device:TPU:16, one launch (start us, length us, event | category | flops | bytes accessed | tf_op | source)
XLA Modules:
  0.0 480.6 jit_solution(14643431343657749393)
XLA Ops:
  0.7 1.2 slice.102
  2.0 3.2 collective-permute-start
  5.2 1.1 copy.298
  6.4 1.2 reshape.149
  7.6 4.8 all-to-all-start
  12.5 4.2 all-to-all-done
  17.3 1.4 reduce
  19.4 1.0 reshape.148
  20.4 12.6 %all-to-all-start.1 = ((f32[1,64,4,256]{3,2,0,1:T(4,128)}), f32[1,64,4,256]{3,2,0,1:T(4,128)S(1)}, u32[]{:S(2)}, u32[]{:S(2)}) async-start(f32[1,64,4,256]{3,2,0,1:T(4,128)} %reshape.148), calls=%async_computation.1 | async-start | bytes 524288 | tf_op jit(solution)/shard_map/all_to_all | solution.py:130
  34.6 2.5 multiply_add_fusion
  37.1 1.5 pad_maximum_fusion.2
  38.6 6.6 %all-to-all-done.1 = f32[1,64,4,256]{3,2,0,1:T(4,128)S(1)} async-done(((f32[1,64,4,256]{3,2,0,1:T(4,128)}), f32[1,64,4,256]{3,2,0,1:T(4,128)S(1)}, u32[]{:S(2)}, u32[]{:S(2)}) %all-to-all-start.1) | async-done | bytes 262176 | tf_op jit(solution)/shard_map/all_to_all | solution.py:130
  45.2 6.2 %all-to-all-start.2 = ((f32[4,256,256]{2,0,1:T(4,128)}), f32[4,256,256]{2,0,1:T(4,128)S(1)}, u32[]{:S(2)}, u32[]{:S(2)}) async-start(f32[4,256,256]{2,0,1:T(4,128)} %pad_maximum_fusion.2), calls=%async_computation.2 | async-start | bytes 2097152 | tf_op jit(solution)/shard_map/all_to_all | solution.py:138
  54.0 25.6 %all-to-all-done.2 = f32[4,256,256]{2,0,1:T(4,128)S(1)} async-done(((f32[4,256,256]{2,0,1:T(4,128)}), f32[4,256,256]{2,0,1:T(4,128)S(1)}, u32[]{:S(2)}, u32[]{:S(2)}) %all-to-all-start.2) | async-done | bytes 1048608 | tf_op jit(solution)/shard_map/all_to_all | solution.py:138
  83.0 1.6 convolution_bitcast_fusion
  85.4 1.6 fusion.1
  86.9 1.6 convolution_bitcast_fusion.1
  88.5 2.0 fusion.96
  90.5 2.0 fusion.100
  92.5 2.0 fusion.88
  94.5 2.2 fusion.90
  96.8 2.0 fusion.98
  98.8 2.0 fusion.102
  100.8 1.8 squeeze.15
  102.6 1.8 squeeze.16
  104.3 2.3 convolution_subtract_fusion.4
  106.7 1.2 convolution_add_fusion.4
  107.9 1.2 convolution_subtract_fusion.2
  109.1 1.2 convolution_add_fusion.2
  110.4 1.2 convolution_add_fusion.5
  111.6 1.4 multiply_subtract_fusion.3
  113.9 1.3 fusion.92
  117.5 1.3 fusion.4
  118.8 1.1 copy.325
  131.6 20.5 %copy.343 = f32[4,4,16384]{1,0,2:T(4,128)} copy(f32[4,4,16384]{2,1,0:T(4,128)S(1)} %pad_maximum_fusion.3) | data formatting | bytes 2097152 | tf_op jit(solution)/shard_map/stack | solution.py:144
  152.1 40.5 %reshape.151 = f32[64,1,4096]{2,1,0:T(1,128)S(1)} reshape(f32[16384,4,4]{2,1,0:T(4,128)} %bitcast.145) | data formatting | bytes 2097152
  192.6 34.2 %all_to_all.63 = f32[64,1,4096]{2,1,0:T(1,128)S(1)} all-to-all(f32[64,1,4096]{2,1,0:T(1,128)S(1)} %reshape.151), channel_id=1, replica_groups=mesh['ctx'=64,'tp'=4] {'ctx'}, dimensions={0} | all-to-all | bytes 2097152 | tf_op jit(solution)/shard_map/all_to_all | solution.py:152
  226.7 3.3 reduce.1
  230.0 45.5 %reshape.152 = f32[16384,4,4]{2,1,0:T(4,128)} reshape(f32[64,4096]{1,0:T(8,128)S(1)} %reduce.1) | data formatting | bytes 2097152
  275.5 24.2 %copy.344 = f32[4,4,64,256]{3,1,2,0:T(4,128)S(1)} copy(f32[4,4,64,256]{1,0,3,2:T(4,128)} %bitcast.146) | data formatting | bytes 2097152 | tf_op jit(solution)/shard_map/all_to_all | solution.py:152
  302.1 1.2 copy.346
  303.3 1.5 collective-permute-start.1
  304.8 1.8 fusion.53
  306.6 2.4 collective-permute-done.1
  309.0 1.7 copy.347
  310.7 8.9 %multiply_reduce_fusion.1 = (f32[3,256]{0,1:T(8,128)}, f32[3,256]{0,1:T(8,128)}, f32[3,256]{0,1:T(8,128)}, f32[3,256,256]{2,0,1:T(4,128)}) fusion(f32[3,256,256]{2,0,1:T(4,128)S(1)} %bitcast.148, f32[3,256,256]{2,0,1:T(4,128)S(1)} %copy-done.1, f32[3,256,2]{2,0,1:T(4,128)S(1)} %copy-done.5, f32[3,256,256]{2,1,0:T(8,128)S(1)} %copy-done.3, ...), kind=kLoop, calls=%fused_computation.46 | loop fusion | flops 2946816 | bytes 3176448 | tf_op jit(solution)/shard_map/reduce_sum | solution.py:161
  319.6 1.1 copy.350
  322.6 155.9 %all-gather = f32[192,3,256]{2,1,0:T(4,128)S(1)} all-gather(f32[3,3,256]{2,1,0:T(4,128)S(1)} %pad_maximum_fusion.4), channel_id=2, replica_groups=mesh['ctx'=64,'tp'=4] {'ctx'}, dimensions={0}, use_global_device_ids=true | all-gather | bytes 599040 | tf_op jit(solution)/shard_map/all_gather | solution.py:9
  (126 shorter events, 30.6 us)
Async XLA Ops:
  0.6 11.8 %copy-start.30 = (f32[256]{0:T(256)S(1)}, f32[256]{0:T(256)}, u32[]{:S(2)}) copy-start(f32[256]{0:T(256)} %param.7) | copy-start | bytes 3076
  0.6 11.8 %copy-start.28 = (f32[256,256]{1,0:T(8,128)S(1)}, f32[256,256]{1,0:T(8,128)}, u32[]{:S(2)}) copy-start(f32[256,256]{1,0:T(8,128)} %param.6) | copy-start | bytes 786436
  2.0 32.3 %collective-permute-start = (f32[3,256,2]{1,0,2:T(4,128)S(1)}, f32[3,256,2]{1,0,2:T(4,128)S(1)}, u32[]{:S(2)}, u32[]{:S(2)}) collective-permute-start(f32[3,256,2]{1,0,2:T(4,128)S(1)} %copy.392), channel_id=1, source_target_pairs={{0,4},{4,8},{8,12},{12,16},{16,20},{20,24},{24,28},{28,32},{32,36}... | collective-permute-start | bytes 18440 | tf_op jit(solution)/shard_map/ppermute | solution.py:16
  7.6 9.2 %all-to-all-start = ((f32[4,1,16384]{2,1,0:T(1,128)}), f32[4,1,16384]{2,1,0:T(1,128)S(1)}, u32[]{:S(2)}, u32[]{:S(2)}) async-start(f32[4,1,16384]{2,1,0:T(1,128)} %reshape.149), calls=%async_computation | async-start | bytes 524288 | tf_op jit(solution)/shard_map/all_to_all | solution.py:131
  18.6 14.4 %copy-start.29 = (f32[3,3,256]{2,1,0:T(4,128)S(1)}, f32[3,3,256]{2,1,0:T(4,128)}, u32[]{:S(2)}) copy-start(f32[3,3,256]{2,1,0:T(4,128)} %param.8) | copy-start | bytes 27652
  18.7 14.4 %copy-start.2 = (f32[3,256,256]{2,1,0:T(8,128)S(1)}, f32[3,256,256]{2,1,0:T(8,128)}, u32[]{:S(2)}) copy-start(f32[3,256,256]{2,1,0:T(8,128)} %param.5) | copy-start | bytes 2359300
  20.4 24.7 %all-to-all-start.1 = ((f32[1,64,4,256]{3,2,0,1:T(4,128)}), f32[1,64,4,256]{3,2,0,1:T(4,128)S(1)}, u32[]{:S(2)}, u32[]{:S(2)}) async-start(f32[1,64,4,256]{3,2,0,1:T(4,128)} %reshape.148), calls=%async_computation.1 | async-start | bytes 524288 | tf_op jit(solution)/shard_map/all_to_all | solution.py:130
  33.6 3.5 copy-start
  33.9 3.2 copy-start.22
  34.1 3.1 copy-start.23
  34.6 4.0 copy-start.4
  45.2 8.7 %copy-start.14 = (f32[1,64,4,256]{3,2,0,1:T(4,128)}, f32[1,64,4,256]{3,2,0,1:T(4,128)S(1)}, u32[]{:S(2)}) copy-start(f32[1,64,4,256]{3,2,0,1:T(4,128)S(1)} %all-to-all-done.1) | copy-start | bytes 786436
  45.2 34.4 %all-to-all-start.2 = ((f32[4,256,256]{2,0,1:T(4,128)}), f32[4,256,256]{2,0,1:T(4,128)S(1)}, u32[]{:S(2)}, u32[]{:S(2)}) async-start(f32[4,256,256]{2,0,1:T(4,128)} %pad_maximum_fusion.2), calls=%async_computation.2 | async-start | bytes 2097152 | tf_op jit(solution)/shard_map/all_to_all | solution.py:138
  52.3 30.7 %copy-start.7 = (f32[256,256]{1,0:T(8,128)}, f32[256,256]{1,0:T(8,128)S(1)}, u32[]{:S(2)}) copy-start(f32[256,256]{1,0:T(8,128)S(1)} %fusion.61) | copy-start | bytes 786436
  53.3 32.0 %copy-start.11 = (f32[256,256]{1,0:T(8,128)}, f32[256,256]{1,0:T(8,128)S(1)}, u32[]{:S(2)}) copy-start(f32[256,256]{1,0:T(8,128)S(1)} %fusion.60) | copy-start | bytes 786436
  81.1 1.3 copy-start.16
  82.4 2.2 copy-start.27
  104.3 2.3 copy-start.20
  106.7 1.2 copy-start.19
  107.9 1.2 copy-start.17
  109.1 1.2 copy-start.18
  110.4 1.2 copy-start.21
  115.1 1.8 copy-start.8
  116.0 1.5 copy-start.12
  122.5 1.8 copy-start.9
  123.3 1.5 copy-start.13
  127.5 1.8 copy-start.10
  130.0 1.0 copy-start.15
  130.0 1.0 copy-start.26
  130.1 1.1 copy-start.24
  130.1 1.2 copy-start.25
  301.2 9.5 %copy-start.1 = (f32[3,256,256]{2,0,1:T(4,128)S(1)}, f32[3,256,256]{2,0,1:T(4,128)}, u32[]{:S(2)}) copy-start(f32[3,256,256]{2,0,1:T(4,128)} %copy-done) | copy-start | bytes 2359300
  301.2 9.5 %copy-start.3 = (f32[3,256,256]{2,1,0:T(8,128)S(1)}, f32[3,256,256]{2,1,0:T(8,128)}, u32[]{:S(2)}) copy-start(f32[3,256,256]{2,1,0:T(8,128)} %param.5) | copy-start | bytes 2359300
  301.2 9.5 %copy-start.5 = (f32[3,256,2]{2,0,1:T(4,128)S(1)}, f32[3,256,2]{2,0,1:T(4,128)}, u32[]{:S(2)}) copy-start(f32[3,256,2]{2,0,1:T(4,128)} %copy-done.4) | copy-start | bytes 18436
  303.3 5.7 %collective-permute-start.1 = (f32[3,256,2]{1,0,2:T(4,128)S(1)}, f32[3,256,2]{1,0,2:T(4,128)}, u32[]{:S(2)}, u32[]{:S(2)}) collective-permute-start(f32[3,256,2]{1,0,2:T(4,128)S(1)} %copy.346), channel_id=1, source_target_pairs={{4,0},{8,4},{12,8},{16,12},{20,16},{24,20},{28,24},{32,28},{36,32}... | collective-permute-start | bytes 18440 | tf_op jit(solution)/shard_map/ppermute | solution.py:16
  319.6 159.8 %copy-start.6 = (f32[3,256,256]{2,0,1:T(4,128)S(1)}, f32[3,256,256]{2,0,1:T(4,128)}, u32[]{:S(2)}) copy-start(f32[3,256,256]{2,0,1:T(4,128)} %get-tuple-element.27) | copy-start | bytes 2359300
